TPU v7x, 32 devices: a whole 2x2x4 slice. The times are simulated.
32 devices in a mesh: gx: 8 (over y, x, core), gz: 4 (over z).
Axes of the slice: x: 2, y: 2, z: 4, core: 2. Of those that a mesh axis runs over, the one named last changes fastest.
Arguments:
- pressure_now: float32 [128, 128, 512], P('gz', 'gx'), may hold values from -6 to 6
- pressure_prev: float32 [128, 128, 512], P('gz', 'gx'), may hold values from -6 to 6
- adjoint_now: float32 [128, 128, 512], P('gz', 'gx'), may hold values from -6 to 6
- adjoint_prev: float32 [128, 128, 512], P('gz', 'gx'), may hold values from -6 to 6
- speed2: float32 [128, 128, 512], P('gz', 'gx'), may hold values from 0.05 to 0.32
- layer_state: float32 [4096, 64, 128], P(('gx', 'gz')), may hold values from -3 to 3
- layer_maps: float32 [8, 64, 64], replicated, as said below
- send_rows: int32 [32, 32, 4], P(('gx', 'gz')), may hold values from -1 to 2047, as said below
- slot_patch: int32 [4096], P(('gx', 'gz')), may hold values from 0 to 255
- patch_material: int32 [256], replicated, may hold values from 0 to 7
Outputs:
- pressure_out: float32 [128, 128, 512], P('gz', 'gx')
- adjoint_out: float32 [128, 128, 512], P('gz', 'gx')
- patch_gradient: float32 [256, 128], P(('gx', 'gz'))
Inputs may be any that keep to these rules, and one draw needn't show every extreme that they name: `send_rows`: each device's non-negative entries are distinct rows of its tile; -1 marks an unused entry; for one device every entry aimed at it is used. `layer_maps`: each material's matrix has diagonal entries from 0.5 to 0.9.
All inputs are finite; a program needn't handle non-finite values.
Results may differ from a plain program's by a relative error of at most 0.00016.
Values sent between devices are 32-bit elements; how exact they have to be, the bound alone decides.
A program may use at most 192 MiB of HBM per device.

v0:
```python
import functools

import jax
import jax.numpy as jnp
from jax import lax
from jax.experimental import pallas as pl
from jax.experimental.pallas import tpu as pltpu
from jax.sharding import PartitionSpec as P

STEPS = 4
KAPPA = 0.5
BETA = 0.3
TERMS = STEPS + 1
LANES = 128
CHUNK = 16
ORDER = (("a", 0), ("a", 1), ("p", 0), ("a", 2), ("p", 1), ("a", 3), ("p", 2), ("p", 3))
F32 = jnp.float32
BF16 = jnp.bfloat16
MESH = pl.DeviceIdType.MESH


def split(value):
    high = value.astype(BF16)
    return high, (value - high.astype(F32)).astype(BF16)


def kernel_body(
    nx, nz,
    patch_s, material_s, rows_s, maps, src_lane, src_column,
    p_now_h, p_prev_h, a_now_h, a_prev_h, speed2_h, state_h,
    p_out, a_out, grad_out,
    p_now, p_prev, p_mid, a_now, a_prev, a_mid, speed2, state,
    spread, couple, hist, weights, chain, table, ctab,
    info_send, info_recv, info, relay_send, relay_recv, surf, backs, scale,
    grad_send, grad_recv, x_send, x_recv, z_recv,
    load_sem, chunk_sem, send_sem, recv_sem,
    info_ssem, info_rsem, relay_ssem, relay_rsem, grad_ssem, grad_rsem,
):
    cz, blocks, cx, _ = speed2.shape
    slots = src_lane.shape[1]
    devices = nx * nz
    cap = slots // devices
    mats, depth, _ = maps.shape
    patches = material_s.shape[0]
    own = patches // devices
    chunks = slots // CHUNK
    peers = CHUNK // cap

    gx, gz = lax.axis_index("gx"), lax.axis_index("gz")
    me = gx * nz + gz
    exists = [gx > 0, gx < nx - 1, gz > 0, gz < nz - 1]
    target = [(gx - 1, gz), (gx + 1, gz), (gx, gz - 1), (gx, gz + 1)]

    def where_is(flat):
        return (lax.div(flat, nz), lax.rem(flat, nz))

    first_chunk = lax.div(me * cap, CHUNK)
    loads = {}
    for i, (name, src, dst) in enumerate((
        ("a", a_now_h, a_now), ("p", p_now_h, p_now),
        ("ap", a_prev_h, a_prev), ("s", speed2_h, speed2), ("pp", p_prev_h, p_prev),
    )):
        loads[name] = [
            pltpu.make_async_copy(
                src.at[:, :, pl.ds(rb * LANES, LANES)], dst.at[:, rb], load_sem.at[i, rb]
            )
            for rb in range(blocks)
        ]

    def chunk_copy(j):
        at = lax.rem(first_chunk + j, chunks) * CHUNK
        return pltpu.make_async_copy(
            state_h.at[pl.ds(at, CHUNK)], state.at[pl.ds(at, CHUNK)], chunk_sem.at[j]
        )

    barrier = pltpu.get_barrier_semaphore()

    @pl.loop(1, devices)
    def _(o):
        pl.semaphore_signal(
            barrier, inc=1, device_id=where_is(lax.rem(me + o, devices)), device_id_type=MESH
        )

    for name in ("a", "p"):
        for copy in loads[name]:
            copy.start()

    @pl.loop(0, chunks)
    def _(j):
        chunk_copy(j).start()

    for name in ("ap", "s", "pp"):
        for copy in loads[name]:
            copy.start()

    row8 = lax.broadcasted_iota(jnp.int32, (mats, LANES), 0)
    lane8 = lax.broadcasted_iota(jnp.int32, (mats, LANES), 1)
    halve = jnp.where(lane8 % depth == 0, 1.0 - KAPPA, 1.0)
    for j in range(mats // 2):
        high, low = split(jnp.concatenate([maps[2 * j], maps[2 * j + 1]], axis=1))
        weights[:, j * LANES : (j + 1) * LANES] = jnp.concatenate([high, low, high, low], axis=0)
    v = jnp.concatenate([maps[m, 0:1, :] for m in range(mats)], axis=0)
    v = jnp.concatenate([v, v], axis=1) * halve
    coefs = jnp.zeros((mats, LANES), F32)
    for n in range(TERMS):
        chain[n] = v
        coefs = jnp.where(lane8 == n, v[:, 0:1] * (KAPPA / (1.0 - KAPPA)), coefs)
        if n < TERMS - 1:
            high, low = split(v)
            got = jnp.dot(
                jnp.concatenate([high, low], axis=1), weights[...], preferred_element_type=F32
            )
            total = jnp.zeros((mats, LANES), F32)
            for j in range(mats // 2):
                keep = 2 * j + lane8 // depth == row8
                total = total + jnp.where(keep, got[:, j * LANES : (j + 1) * LANES], 0.0)
            v = (total + pltpu.roll(total, depth, 1)) * halve
    ctab[...] = coefs
    low_half = lax.broadcasted_iota(jnp.int32, (8, LANES), 1) < depth
    for m in range(mats):
        rows = jnp.concatenate(
            [chain[n, m : m + 1, :] for n in range(TERMS)] + [jnp.zeros((8 - TERMS, LANES), F32)],
            axis=0,
        )
        high = rows.astype(BF16)
        low = jnp.where(low_half, rows - high.astype(F32), 0.0).astype(BF16)
        table[m] = jnp.concatenate([high, low], axis=0)

    lane1 = lax.broadcasted_iota(jnp.int32, (1, LANES), 1)

    @pl.loop(0, devices)
    def _(k):
        for c in range(cap):
            patch = patch_s[k * cap + c]
            coef = ctab[pl.ds(material_s[patch], 1), :]
            ids = jnp.full((1, LANES), patch, jnp.int32).astype(F32)
            info_send[k, c : c + 1, :] = jnp.where(lane1 == TERMS, ids, coef)

    now = {"p": p_now, "a": a_now}
    buffers = {"p": (p_prev, p_now, p_mid), "a": (a_prev, a_now, a_mid)}
    outs = {"p": p_out, "a": a_out}
    which = {"p": 0, "a": 1}

    def halo_copy(name, step, d, source):
        field = which[name]
        if d < 2:
            ref, dst = x_send.at[step, field, d], x_recv.at[step, field, 1 - d]
        else:
            ref = source.at[0 if d == 2 else cz - 1]
            dst = z_recv.at[step, field, 3 - d]
        return pltpu.make_async_remote_copy(
            src_ref=ref, dst_ref=dst,
            send_sem=send_sem.at[step, field, d],
            recv_sem=recv_sem.at[step, field, d ^ 1],
            device_id=target[d], device_id_type=MESH,
        )

    def start_halo(name, step, source):
        for d in range(4):
            @pl.when(exists[d])
            def _(d=d):
                halo_copy(name, step, d, source).start()

    def wait_recv(name, step):
        field = which[name]
        for d in range(4):
            @pl.when(exists[d])
            def _(d=d):
                side = x_recv.at[step, field, d] if d < 2 else z_recv.at[step, field, d - 2]
                pltpu.make_async_remote_copy(
                    src_ref=side, dst_ref=side,
                    send_sem=send_sem.at[step, field, d],
                    recv_sem=recv_sem.at[step, field, d],
                    device_id=target[d], device_id_type=MESH,
                ).wait_recv()

    def wait_send(name, step, source):
        for d in range(4):
            @pl.when(exists[d])
            def _(d=d):
                halo_copy(name, step, d, source).wait_send()

    for d in range(4):
        @pl.when(jnp.logical_not(exists[d]))
        def _(d=d):
            for step in range(STEPS):
                for field in range(2):
                    if d < 2:
                        x_recv[step, field, d] = jnp.zeros((cz, blocks, LANES), F32)
                    else:
                        z_recv[step, field, d - 2] = jnp.zeros((blocks, cx, LANES), F32)

    lanes = src_lane[...]
    xrow = lax.broadcasted_iota(jnp.int32, (cx, slots), 0)

    @pl.loop(0, cz)
    def _(z):
        for rb in range(blocks):
            row = z * (cx * blocks) + xrow * blocks + rb
            hit = jnp.where(row == lanes, 1.0, 0.0).astype(BF16)
            spread[z, rb] = jnp.concatenate([hit, hit], axis=1)

    for name in ("a", "p"):
        for copy in loads[name]:
            copy.wait()

        @pl.loop(0, cz)
        def _(z, name=name):
            for rb in range(blocks):
                x_send[0, which[name], 0, z, rb : rb + 1, :] = now[name][z, rb, 0:1, :]
                x_send[0, which[name], 1, z, rb : rb + 1, :] = now[name][z, rb, cx - 1 : cx, :]

    pl.semaphore_wait(barrier, devices - 1)
    start_halo("a", 0, now["a"])
    start_halo("p", 0, now["p"])

    @pl.loop(1, devices)
    def _(o):
        k = lax.rem(me + o, devices)
        pltpu.make_async_remote_copy(
            src_ref=info_send.at[k], dst_ref=info_recv.at[me],
            send_sem=info_ssem, recv_sem=info_rsem,
            device_id=where_is(k), device_id_type=MESH,
        ).start()

    def relay_copy(k, part):
        rows = pl.ds(0, 1) if part == 0 else pl.ds(1, TERMS - 1)
        return pltpu.make_async_remote_copy(
            src_ref=relay_send.at[k, rows], dst_ref=relay_recv.at[me, rows],
            send_sem=relay_ssem.at[part], recv_sem=relay_rsem.at[part],
            device_id=where_is(k), device_id_type=MESH,
        )

    @pl.loop(0, chunks)
    def _(j):
        chunk = lax.rem(first_chunk + j, chunks)
        chunk_copy(j).wait()
        for pair in range(CHUNK // 2):
            at = chunk * CHUNK + 2 * pair
            mat = [material_s[patch_s[at + i]] for i in range(2)]
            data = jnp.concatenate([state[at], state[at + 1]], axis=1)
            high, low = split(data)
            both = jnp.dot(
                jnp.concatenate([table[mat[0]], table[mat[1]]], axis=0),
                jnp.concatenate([high, low], axis=0), preferred_element_type=F32,
            )
            for i in range(2):
                part = both[16 * i : 16 * i + 16, i * LANES : (i + 1) * LANES]
                got = part[:8] + part[8:]
                slot = 2 * pair + i
                for n in range(TERMS):
                    relay_send[
                        chunk * peers + slot // cap, n, slot % cap : slot % cap + 1, :
                    ] = got[n : n + 1]
        for q in range(peers):
            k = chunk * peers + q
            @pl.when(k != me)
            def _(k=k):
                relay_copy(k, 0).start()
                relay_copy(k, 1).start()

    def gather(source, name, step):
        field = which[name]

        @pl.loop(0, slots // 8)
        def _(b):
            base = pl.multiple_of(b * 8, 8)
            picked = []
            for i in range(8):
                r = jnp.maximum(rows_s[base + i], 0)
                z = lax.div(r, cx * blocks)
                x = lax.rem(lax.div(r, blocks), cx)
                picked.append(source[z, lax.rem(r, blocks), pl.ds(x, 1), :])
            valid = src_column[pl.ds(base, 8), :] >= 0
            hist[field, step, pl.ds(base, 8), :] = jnp.where(
                valid, jnp.concatenate(picked, axis=0), 0.0
            )

    def wait_info():
        side = info_recv.at[pl.ds(0, devices - 1)]
        pltpu.make_async_remote_copy(
            src_ref=side, dst_ref=side, send_sem=info_ssem, recv_sem=info_rsem,
            device_id=where_is(lax.rem(me + 1, devices)), device_id_type=MESH,
        ).wait_recv()
        info_recv[me] = info_send[me]
        for k in range(devices):
            info[k * cap : (k + 1) * cap, :] = info_recv[k]
        for n in range(TERMS):
            scale[n] = jnp.broadcast_to(info[:, n : n + 1], (slots, LANES))

    def wait_relay(part):
        rows = pl.ds(0, 1) if part == 0 else pl.ds(1, TERMS - 1)
        side = relay_recv.at[pl.ds(0, devices - 1), rows]
        pltpu.make_async_remote_copy(
            src_ref=side, dst_ref=side, send_sem=relay_ssem.at[part], recv_sem=relay_rsem.at[part],
            device_id=where_is(lax.rem(me + 1, devices)), device_id_type=MESH,
        ).wait_recv()
        for n in ([0] if part == 0 else range(1, TERMS)):
            relay_recv[me, n] = relay_send[me, n]
            for k in range(devices):
                surf[n, k * cap : (k + 1) * cap, :] = relay_recv[k, n]

    def grad_copy(k):
        return pltpu.make_async_remote_copy(
            src_ref=grad_send.at[k], dst_ref=grad_recv.at[me],
            send_sem=grad_ssem, recv_sem=grad_rsem,
            device_id=where_is(k), device_id_type=MESH,
        )

    def correlate():
        total = jnp.zeros((slots, LANES), F32)
        for t in range(STEPS):
            inner = float(STEPS - t) * surf[STEPS - t]
            for q in range(STEPS - t):
                inner = inner + float(STEPS - t - q) * scale[STEPS - t - q] * hist[0, q]
                inner = inner + scale[STEPS - 1 - t - q] * backs[q]
            total = total + KAPPA * hist[1, t] * inner
        square = lax.broadcasted_iota(jnp.int32, (slots, slots), 0)
        across = lax.broadcasted_iota(jnp.int32, (slots, slots), 1)
        column = jnp.broadcast_to(info[:, TERMS : TERMS + 1], (slots, slots))
        patch = jnp.sum(jnp.where(square == across, column, 0.0), axis=0, keepdims=True)
        which_patch = lax.broadcasted_iota(jnp.int32, (patches, slots), 0)
        owners = jnp.where(which_patch == patch.astype(jnp.int32), 1.0, 0.0).astype(BF16)
        sums = jnp.dot(
            owners, jnp.concatenate(split(total), axis=1), preferred_element_type=F32
        )
        grad_send[...] = (sums[:, :LANES] + sums[:, LANES:]).reshape(devices, own, LANES)

        @pl.loop(1, devices)
        def _(o):
            grad_copy(lax.rem(me + o, devices)).start()
        grad_recv[me] = grad_send[me]

    row_id = lax.broadcasted_iota(jnp.int32, (cx, LANES), 0)
    lane_id = lax.broadcasted_iota(jnp.int32, (cx, LANES), 1)

    gather(now["a"], "a", 0)
    wait_info()
    gather(now["p"], "p", 0)
    waited = {"ap": False, "s": False, "pp": False}
    gathered = {("a", 0), ("p", 0)}
    sent = False

    for name, step in ORDER:
        field = which[name]
        last = step == STEPS - 1
        ring = buffers[name]
        earlier, current = ring[step % 3], ring[(step + 1) % 3]
        result = outs[name] if last else ring[(step + 2) % 3]

        if name == "p" and step < 2:
            wait_relay(step)
        back = surf[step] if name == "p" else jnp.zeros((slots, LANES), F32)
        for t in range(step + 1):
            back = back + scale[step - t] * hist[field, t]
        if name == "p":
            backs[step] = back
            if last:
                correlate()
        delta = BETA * (back - hist[field, step])
        both = jnp.concatenate(split(delta), axis=0)

        @pl.loop(0, 4)
        def _(part):
            span = pl.ds(pl.multiple_of(part * (cz // 4), cz // 4), cz // 4)
            couple[span] = jnp.dot(
                spread[span].reshape(cz // 4 * blocks * cx, 2 * slots), both,
                preferred_element_type=F32,
            ).reshape(cz // 4, blocks, cx, LANES)

        for need in ((name + "p",) if step == 0 else ()) + ("s",):
            if not waited[need]:
                waited[need] = True
                for copy in loads[need]:
                    copy.wait()
        wait_recv(name, step)
        if step > 0:
            wait_send(name, step - 1, earlier)

        def plane(z, down, up):
            f = [current[z, rb] for rb in range(blocks)]
            right = [pltpu.roll(part, 1, 1) for part in f]
            left = [pltpu.roll(part, LANES - 1, 1) for part in f]
            for rb in range(blocks):
                lo = x_recv[step, field, 0, z, rb : rb + 1, :]
                hi = x_recv[step, field, 1, z, rb : rb + 1, :]
                west = jnp.where(row_id == 0, lo, pltpu.roll(f[rb], 1, 0))
                east = jnp.where(row_id == cx - 1, hi, pltpu.roll(f[rb], cx - 1, 0))
                south = jnp.where(lane_id == 0, right[rb - 1] if rb else 0.0, right[rb])
                north = jnp.where(
                    lane_id == LANES - 1, left[rb + 1] if rb < blocks - 1 else 0.0, left[rb]
                )
                beside = (down[rb] + up[rb]) + (west + east) + (south + north)
                new = (2.0 * f[rb] - earlier[z, rb] + couple[z, rb]) + speed2[z, rb] * (
                    beside - 6.0 * f[rb]
                )
                if last:
                    result[z, :, rb * LANES : (rb + 1) * LANES] = new
                else:
                    result[z, rb] = new
                    x_send[step + 1, field, 0, z, rb : rb + 1, :] = new[0:1]
                    x_send[step + 1, field, 1, z, rb : rb + 1, :] = new[cx - 1 : cx]

        plane(0, z_recv.at[step, field, 0], current.at[1])
        plane(cz - 1, current.at[cz - 2], z_recv.at[step, field, 1])

        @pl.loop(1, cz - 1)
        def _(z):
            plane(z, current.at[z - 1], current.at[z + 1])

        if last:
            wait_send(name, step, current)
        else:
            start_halo(name, step + 1, result)
            gather(result, name, step + 1)

    side = grad_recv.at[pl.ds(0, devices - 1)]
    pltpu.make_async_remote_copy(
        src_ref=side, dst_ref=side, send_sem=grad_ssem, recv_sem=grad_rsem,
        device_id=where_is(lax.rem(me + 1, devices)), device_id_type=MESH,
    ).wait_recv()
    grad_out[...] = jnp.sum(grad_recv[...], axis=0)

    for part, sem, buf in (
        (0, grad_ssem, grad_send.at[pl.ds(0, devices - 1)]),
        (0, info_ssem, info_send.at[pl.ds(0, devices - 1)]),
        (0, relay_ssem.at[0], relay_send.at[pl.ds(0, devices - 1), pl.ds(0, 1)]),
        (1, relay_ssem.at[1], relay_send.at[pl.ds(0, devices - 1), pl.ds(1, TERMS - 1)]),
    ):
        pltpu.make_async_remote_copy(
            src_ref=buf, dst_ref=buf, send_sem=sem, recv_sem=grad_rsem,
            device_id=where_is(lax.rem(me + 1, devices)), device_id_type=MESH,
        ).wait_send()


def body(
    nx, nz, pressure_now, pressure_prev, adjoint_now, adjoint_prev, speed2,
    layer_state, layer_maps, send_rows, slot_patch, patch_material,
):
    slots, depth, width = layer_state.shape
    devices = nx * nz
    patches = patch_material.shape[0]
    mats = layer_maps.shape[0]
    cap = slots // devices
    own = patches // devices
    cz, cx, ny = speed2.shape
    src = send_rows.reshape(-1)
    vmem = pl.BlockSpec(memory_space=pltpu.VMEM)
    smem = pl.BlockSpec(memory_space=pltpu.SMEM)
    hbm = pl.BlockSpec(memory_space=pl.ANY)
    dma = pltpu.SemaphoreType.DMA
    blocks = ny // LANES
    tile = pltpu.VMEM((cz, blocks, cx, LANES), F32)
    rows = pltpu.VMEM((devices, cap, width), F32)
    return pl.pallas_call(
        functools.partial(kernel_body, nx, nz),
        out_shape=(
            jax.ShapeDtypeStruct((cz, cx, ny), F32),
            jax.ShapeDtypeStruct((cz, cx, ny), F32),
            jax.ShapeDtypeStruct((own, width), F32),
        ),
        in_specs=[smem] * 3 + [vmem] * 3 + [hbm] * 6,
        out_specs=(vmem, vmem, vmem),
        scratch_shapes=[
            tile, tile, tile, tile, tile, tile, tile,
            pltpu.VMEM((slots, depth, width), F32),
            pltpu.VMEM((cz, blocks, cx, 2 * slots), BF16),
            tile,
            pltpu.VMEM((2, STEPS, slots, LANES), F32),
            pltpu.VMEM((4 * depth, mats * depth), BF16),
            pltpu.VMEM((TERMS, mats, LANES), F32),
            pltpu.VMEM((mats, 16, LANES), BF16),
            pltpu.VMEM((mats, LANES), F32),
            rows, rows,
            pltpu.VMEM((slots, width), F32),
            pltpu.VMEM((devices, TERMS, cap, width), F32),
            pltpu.VMEM((devices, TERMS, cap, width), F32),
            pltpu.VMEM((TERMS, slots, width), F32),
            pltpu.VMEM((STEPS, slots, width), F32),
            pltpu.VMEM((TERMS, slots, width), F32),
            pltpu.VMEM((devices, own, width), F32),
            pltpu.VMEM((devices, own, width), F32),
            pltpu.VMEM((STEPS, 2, 2, cz, blocks, LANES), F32),
            pltpu.VMEM((STEPS, 2, 2, cz, blocks, LANES), F32),
            pltpu.VMEM((STEPS, 2, 2, blocks, cx, LANES), F32),
            dma((5, blocks)), dma((slots // CHUNK,)),
            dma((STEPS, 2, 4)), dma((STEPS, 2, 4)),
            dma, dma, dma((2,)), dma((2,)), dma, dma,
        ],
        compiler_params=pltpu.CompilerParams(
            collective_id=0, has_side_effects=True, vmem_limit_bytes=56 * 1024 * 1024
        ),
    )(
        slot_patch, patch_material, src, layer_maps, src.reshape(1, slots), src.reshape(slots, 1),
        pressure_now, pressure_prev, adjoint_now, adjoint_prev, speed2, layer_state,
    )


def solution(mesh):
    in_specs = (
        P("gz", "gx", None),
        P("gz", "gx", None),
        P("gz", "gx", None),
        P("gz", "gx", None),
        P("gz", "gx", None),
        P(("gx", "gz"), None, None),
        P(),
        P(("gx", "gz"), None, None),
        P(("gx", "gz")),
        P(),
    )
    out_specs = (P("gz", "gx", None), P("gz", "gx", None), P(("gx", "gz"), None))
    return jax.shard_map(
        functools.partial(body, mesh.shape["gx"], mesh.shape["gz"]),
        mesh=mesh, in_specs=in_specs, out_specs=out_specs, check_vma=False,
    )
```

profile of v0, /device:TPU:0, one launch (start us, length us, event | category | flops | bytes accessed | tf_op | source)
XLA Modules:
  0.0 66.7 jit_solution(2064350533627441607)
XLA Ops:
  0.6 0.8 %copy.17 = s32[1,32,4]{2,1,0:T(8,128)S(1)} copy(s32[1,32,4]{1,2,0:T(4,128)} %param.17) | data formatting | bytes 1024 | tf_op args[7]
  1.4 0.6 reshape_reshape.6.src_lane
  2.0 0.6 reshape.9.rows_s
  2.6 0.7 %reshape_reshape.8.src_column = s32[128,1]{1,0:T(8,128)} reshape(s32[1,32,4]{2,1,0:T(8,128)S(1)} %copy.17) | data formatting | bytes 1024 | tf_op jit(solution)/shard_map/reshape;reshape | solution.py:494
  3.3 58.2 %shard_map.121 = (f32[32,16,512]{2,1,0:T(8,128)}, f32[32,16,512]{2,1,0:T(8,128)}, f32[8,128]{1,0:T(8,128)}) custom-call(s32[128]{0:T(128)} %patch_s.1, s32[256]{0:T(256)} %material_s.1, s32[128]{0:T(128)} %reshape.9.rows_s, f32[8,64,64]{2,1,0:T(8,128)} %maps.1, s32[1,128]{1,0:T(1,128)} %reshape_reshape.6.src_lane, s32[128,1]{1,0:T(8,128)} %reshape_reshape.8.src_column, ...), custom_call_target="tpu_custom_call" | custom-call | tf_op jit(solution)/shard_map/pallas_call | solution.py:455
  61.5 0.0 copy-start
  61.5 2.3 %copy.24 = f32[32,16,512]{2,1,0:T(8,128)} copy(f32[32,16,512]{2,1,0:T(8,128)} %get-tuple-element.6) | data formatting | bytes 2097152
  63.8 2.3 %copy.25 = f32[32,16,512]{2,1,0:T(8,128)} copy(f32[32,16,512]{2,1,0:T(8,128)} %get-tuple-element.7) | data formatting | bytes 2097152
  66.2 0.0 copy-done
  66.2 0.6 copy.26
Async XLA Ops:
  61.5 4.6 %copy-start = (f32[8,128]{1,0:T(8,128)S(1)}, f32[8,128]{1,0:T(8,128)}, u32[]{:S(2)}) copy-start(f32[8,128]{1,0:T(8,128)} %get-tuple-element.8) | copy-start | bytes 12292
where the time goes:
time: 67 us; the launch traced here: 66.7 us
  Pallas kernels  58.2 us (87%)
  local copies, waits for them, and re-layouts  7.91 us (12%)
    pallas_call x1, Pallas kernels, body(): pl.pallas_call(functools.partial(kernel_body, nx, nz), out_shape=(jax.Sha...  58.2 us
    unnamed x6, local copies, waits for them, and re-layouts  5.97 us

commit v1 on v0

--- a/solution.py
+++ b/solution.py
@@ -13,7 +13,7 @@
 TERMS = STEPS + 1
 LANES = 128
 CHUNK = 16
-ORDER = (("a", 0), ("a", 1), ("p", 0), ("a", 2), ("p", 1), ("a", 3), ("p", 2), ("p", 3))
+UNROLL = 8
 F32 = jnp.float32
 BF16 = jnp.bfloat16
 MESH = pl.DeviceIdType.MESH
@@ -26,20 +26,19 @@
 
 def kernel_body(
     nx, nz,
-    patch_s, material_s, rows_s, maps, src_lane, src_column,
+    patch_s, material_s, rows_s, maps,
     p_now_h, p_prev_h, a_now_h, a_prev_h, speed2_h, state_h,
     p_out, a_out, grad_out,
     p_now, p_prev, p_mid, a_now, a_prev, a_mid, speed2, state,
-    spread, couple, hist, weights, chain, table, ctab,
+    spread, couple, valid, place, lane_row, hist, weights, chain, table, ctab,
     info_send, info_recv, info, relay_send, relay_recv, surf, backs, scale,
     grad_send, grad_recv, x_send, x_recv, z_recv,
     load_sem, chunk_sem, send_sem, recv_sem,
     info_ssem, info_rsem, relay_ssem, relay_rsem, grad_ssem, grad_rsem,
 ):
     cz, blocks, cx, _ = speed2.shape
-    slots = src_lane.shape[1]
-    devices = nx * nz
-    cap = slots // devices
+    devices, cap = rows_s.shape
+    slots = devices * cap
     mats, depth, _ = maps.shape
     patches = material_s.shape[0]
     own = patches // devices
@@ -62,7 +61,9 @@
     )):
         loads[name] = [
             pltpu.make_async_copy(
-                src.at[:, :, pl.ds(rb * LANES, LANES)], dst.at[:, rb], load_sem.at[i, rb]
+                src.at[:, :, pl.ds(rb * LANES, LANES)],
+                dst.at[:, rb] if name == "s" else dst.at[pl.ds(1, cz), rb],
+                load_sem.at[i, rb],
             )
             for rb in range(blocks)
         ]
@@ -127,6 +128,22 @@
         table[m] = jnp.concatenate([high, low], axis=0)
 
     lane1 = lax.broadcasted_iota(jnp.int32, (1, LANES), 1)
+    slot_lane = lax.broadcasted_iota(jnp.int32, (1, slots), 1)
+    bit_b, bit_x = blocks.bit_length() - 1, cx.bit_length() - 1
+
+    def index_rows(k, row):
+        for c in range(cap):
+            raw = rows_s[k, c]
+            row = jnp.where(slot_lane == k * cap + c, raw, row)
+            r = jnp.maximum(raw, 0)
+            z = lax.shift_right_logical(r, bit_b + bit_x)
+            x = lax.shift_right_logical(r, bit_b) & (cx - 1)
+            place[k * cap + c] = ((z + 1) * blocks + (r & (blocks - 1))) * cx + x
+        return row
+
+    lane_row[...] = lax.fori_loop(
+        0, devices, index_rows, jnp.full((1, slots), -1, jnp.int32), unroll=4
+    )
 
     @pl.loop(0, devices)
     def _(k):
@@ -146,7 +163,7 @@
         if d < 2:
             ref, dst = x_send.at[step, field, d], x_recv.at[step, field, 1 - d]
         else:
-            ref = source.at[0 if d == 2 else cz - 1]
+            ref = source.at[1 if d == 2 else cz]
             dst = z_recv.at[step, field, 3 - d]
         return pltpu.make_async_remote_copy(
             src_ref=ref, dst_ref=dst,
@@ -190,16 +207,6 @@
                     else:
                         z_recv[step, field, d - 2] = jnp.zeros((blocks, cx, LANES), F32)
 
-    lanes = src_lane[...]
-    xrow = lax.broadcasted_iota(jnp.int32, (cx, slots), 0)
-
-    @pl.loop(0, cz)
-    def _(z):
-        for rb in range(blocks):
-            row = z * (cx * blocks) + xrow * blocks + rb
-            hit = jnp.where(row == lanes, 1.0, 0.0).astype(BF16)
-            spread[z, rb] = jnp.concatenate([hit, hit], axis=1)
-
     for name in ("a", "p"):
         for copy in loads[name]:
             copy.wait()
@@ -207,8 +214,8 @@
         @pl.loop(0, cz)
         def _(z, name=name):
             for rb in range(blocks):
-                x_send[0, which[name], 0, z, rb : rb + 1, :] = now[name][z, rb, 0:1, :]
-                x_send[0, which[name], 1, z, rb : rb + 1, :] = now[name][z, rb, cx - 1 : cx, :]
+                x_send[0, which[name], 0, z, rb : rb + 1, :] = now[name][z + 1, rb, 0:1, :]
+                x_send[0, which[name], 1, z, rb : rb + 1, :] = now[name][z + 1, rb, cx - 1 : cx, :]
 
     pl.semaphore_wait(barrier, devices - 1)
     start_halo("a", 0, now["a"])
@@ -261,19 +268,14 @@
 
     def gather(source, name, step):
         field = which[name]
-
-        @pl.loop(0, slots // 8)
+        flat = source.reshape((cz + 2) * blocks * cx, LANES)
+
+        @pl.loop(0, slots // 8, unroll=4)
         def _(b):
             base = pl.multiple_of(b * 8, 8)
-            picked = []
-            for i in range(8):
-                r = jnp.maximum(rows_s[base + i], 0)
-                z = lax.div(r, cx * blocks)
-                x = lax.rem(lax.div(r, blocks), cx)
-                picked.append(source[z, lax.rem(r, blocks), pl.ds(x, 1), :])
-            valid = src_column[pl.ds(base, 8), :] >= 0
+            picked = [flat[pl.ds(place[base + i], 1), :] for i in range(8)]
             hist[field, step, pl.ds(base, 8), :] = jnp.where(
-                valid, jnp.concatenate(picked, axis=0), 0.0
+                valid[pl.ds(base, 8), :] > 0.0, jnp.concatenate(picked, axis=0), 0.0
             )
 
     def wait_info():
@@ -307,7 +309,14 @@
             device_id=where_is(k), device_id_type=MESH,
         )
 
+    def back_rows(name, step):
+        back = surf[step] if name == "p" else jnp.zeros((slots, LANES), F32)
+        for t in range(step + 1):
+            back = back + scale[step - t] * hist[which[name], t]
+        return back
+
     def correlate():
+        backs[STEPS - 1] = back_rows("p", STEPS - 1)
         total = jnp.zeros((slots, LANES), F32)
         for t in range(STEPS):
             inner = float(STEPS - t) * surf[STEPS - t]
@@ -315,8 +324,6 @@
                 inner = inner + float(STEPS - t - q) * scale[STEPS - t - q] * hist[0, q]
                 inner = inner + scale[STEPS - 1 - t - q] * backs[q]
             total = total + KAPPA * hist[1, t] * inner
-        square = lax.broadcasted_iota(jnp.int32, (slots, slots), 0)
-        across = lax.broadcasted_iota(jnp.int32, (slots, slots), 1)
         column = jnp.broadcast_to(info[:, TERMS : TERMS + 1], (slots, slots))
         patch = jnp.sum(jnp.where(square == across, column, 0.0), axis=0, keepdims=True)
         which_patch = lax.broadcasted_iota(jnp.int32, (patches, slots), 0)
@@ -331,6 +338,21 @@
             grad_copy(lax.rem(me + o, devices)).start()
         grad_recv[me] = grad_send[me]
 
+    lanes = lane_row[...]
+    square = lax.broadcasted_iota(jnp.int32, (slots, slots), 0)
+    across = lax.broadcasted_iota(jnp.int32, (slots, slots), 1)
+    used = jnp.where(lanes >= 0, 1.0, 0.0)
+    column = jnp.sum(jnp.where(square == across, used, 0.0), axis=1, keepdims=True)
+    valid[...] = jnp.broadcast_to(column, (slots, LANES))
+    xrow = lax.broadcasted_iota(jnp.int32, (cx, slots), 0)
+
+    @pl.loop(0, cz)
+    def _(z):
+        for rb in range(blocks):
+            row = z * (cx * blocks) + xrow * blocks + rb
+            hit = jnp.where(row == lanes, 1.0, 0.0).astype(BF16)
+            spread[z, rb] = jnp.concatenate([hit, hit], axis=1)
+
     row_id = lax.broadcasted_iota(jnp.int32, (cx, LANES), 0)
     lane_id = lax.broadcasted_iota(jnp.int32, (cx, LANES), 1)
 
@@ -341,7 +363,7 @@
     gathered = {("a", 0), ("p", 0)}
     sent = False
 
-    for name, step in ORDER:
+    for step, name in [(step, name) for step in range(STEPS) for name in ("a", "p")]:
         field = which[name]
         last = step == STEPS - 1
         ring = buffers[name]
@@ -350,17 +372,18 @@
 
         if name == "p" and step < 2:
             wait_relay(step)
-        back = surf[step] if name == "p" else jnp.zeros((slots, LANES), F32)
-        for t in range(step + 1):
-            back = back + scale[step - t] * hist[field, t]
+        if last and name == "a":
+            correlate()
+        if last and name == "p":
+            back = backs[step]
+        else:
+            back = back_rows(name, step)
         if name == "p":
             backs[step] = back
-            if last:
-                correlate()
         delta = BETA * (back - hist[field, step])
         both = jnp.concatenate(split(delta), axis=0)
 
-        @pl.loop(0, 4)
+        @pl.loop(0, 4, unroll=True)
         def _(part):
             span = pl.ds(pl.multiple_of(part * (cz // 4), cz // 4), cz // 4)
             couple[span] = jnp.dot(
@@ -377,8 +400,12 @@
         if step > 0:
             wait_send(name, step - 1, earlier)
 
-        def plane(z, down, up):
-            f = [current[z, rb] for rb in range(blocks)]
+        current[0] = z_recv[step, field, 0]
+        current[cz + 1] = z_recv[step, field, 1]
+
+        @pl.loop(0, cz, unroll=UNROLL)
+        def _(z):
+            f = [current[z + 1, rb] for rb in range(blocks)]
             right = [pltpu.roll(part, 1, 1) for part in f]
             left = [pltpu.roll(part, LANES - 1, 1) for part in f]
             for rb in range(blocks):
@@ -390,23 +417,16 @@
                 north = jnp.where(
                     lane_id == LANES - 1, left[rb + 1] if rb < blocks - 1 else 0.0, left[rb]
                 )
-                beside = (down[rb] + up[rb]) + (west + east) + (south + north)
-                new = (2.0 * f[rb] - earlier[z, rb] + couple[z, rb]) + speed2[z, rb] * (
+                beside = (current[z, rb] + current[z + 2, rb]) + (west + east) + (south + north)
+                new = (2.0 * f[rb] - earlier[z + 1, rb] + couple[z, rb]) + speed2[z, rb] * (
                     beside - 6.0 * f[rb]
                 )
                 if last:
                     result[z, :, rb * LANES : (rb + 1) * LANES] = new
                 else:
-                    result[z, rb] = new
+                    result[z + 1, rb] = new
                     x_send[step + 1, field, 0, z, rb : rb + 1, :] = new[0:1]
                     x_send[step + 1, field, 1, z, rb : rb + 1, :] = new[cx - 1 : cx]
-
-        plane(0, z_recv.at[step, field, 0], current.at[1])
-        plane(cz - 1, current.at[cz - 2], z_recv.at[step, field, 1])
-
-        @pl.loop(1, cz - 1)
-        def _(z):
-            plane(z, current.at[z - 1], current.at[z + 1])
 
         if last:
             wait_send(name, step, current)
@@ -444,13 +464,13 @@
     cap = slots // devices
     own = patches // devices
     cz, cx, ny = speed2.shape
-    src = send_rows.reshape(-1)
     vmem = pl.BlockSpec(memory_space=pltpu.VMEM)
     smem = pl.BlockSpec(memory_space=pltpu.SMEM)
-    hbm = pl.BlockSpec(memory_space=pl.ANY)
+    hbm = pl.BlockSpec(memory_space=pltpu.HBM)
     dma = pltpu.SemaphoreType.DMA
     blocks = ny // LANES
     tile = pltpu.VMEM((cz, blocks, cx, LANES), F32)
+    halo = pltpu.VMEM((cz + 2, blocks, cx, LANES), F32)
     rows = pltpu.VMEM((devices, cap, width), F32)
     return pl.pallas_call(
         functools.partial(kernel_body, nx, nz),
@@ -459,13 +479,16 @@
             jax.ShapeDtypeStruct((cz, cx, ny), F32),
             jax.ShapeDtypeStruct((own, width), F32),
         ),
-        in_specs=[smem] * 3 + [vmem] * 3 + [hbm] * 6,
+        in_specs=[smem] * 3 + [vmem] + [hbm] * 6,
         out_specs=(vmem, vmem, vmem),
         scratch_shapes=[
-            tile, tile, tile, tile, tile, tile, tile,
+            halo, halo, halo, halo, halo, halo, tile,
             pltpu.VMEM((slots, depth, width), F32),
             pltpu.VMEM((cz, blocks, cx, 2 * slots), BF16),
             tile,
+            pltpu.VMEM((slots, LANES), F32),
+            pltpu.SMEM((slots,), jnp.int32),
+            pltpu.VMEM((1, slots), jnp.int32),
             pltpu.VMEM((2, STEPS, slots, LANES), F32),
             pltpu.VMEM((4 * depth, mats * depth), BF16),
             pltpu.VMEM((TERMS, mats, LANES), F32),
@@ -488,10 +511,10 @@
             dma, dma, dma((2,)), dma((2,)), dma, dma,
         ],
         compiler_params=pltpu.CompilerParams(
-            collective_id=0, has_side_effects=True, vmem_limit_bytes=56 * 1024 * 1024
+            collective_id=0, has_side_effects=True, vmem_limit_bytes=51 * 1024 * 1024
         ),
     )(
-        slot_patch, patch_material, src, layer_maps, src.reshape(1, slots), src.reshape(slots, 1),
+        slot_patch, patch_material, send_rows.reshape(devices, cap), layer_maps,
         pressure_now, pressure_prev, adjoint_now, adjoint_prev, speed2, layer_state,
     )
 

time: 67 us -> 43.3 us (0.65)
  Pallas kernels: 58.2 us -> 36.9 us
  local copies, waits for them, and re-layouts: 7.91 us -> 5.58 us
    pallas_call x1, Pallas kernels: 58.2 us -> 36.9 us  [body(): pl.pallas_call(functools.partial(kernel_body, nx, nz), out_shape=(jax.Sha...]
    another operation x2 -> x0, local copies, waits for them, and re-layouts: 1.33 us -> none  [the longest x1 0.71 us: body(): src.reshape(slots, 1)]
    unnamed x6 -> x9, local copies, waits for them, and re-layouts: 5.97 us -> 4.82 us
where the time goes in v1:
time: 43.3 us; the launch traced here: 43.1 us
  Pallas kernels  36.9 us (85%)
  local copies, waits for them, and re-layouts  5.58 us (13%)
  between operations  0.64 us (1%)
    pallas_call x1, Pallas kernels, body(): pl.pallas_call(functools.partial(kernel_body, nx, nz), out_shape=(jax.Sha...  36.9 us
    unnamed x9, local copies, waits for them, and re-layouts  4.82 us

profile of v1, /device:TPU:0, one launch (start us, length us, event | category | flops | bytes accessed | tf_op | source)
XLA Modules:
  0.0 43.1 jit_solution(4634986161268787167)
XLA Ops:
  0.6 0.8 %copy.13.rows_s = s32[32,4]{1,0:T(8,128)S(1)} copy(s32[32,4]{0,1:T(4,128)} %bitcast.1) | data formatting | bytes 1024 | tf_op jit(solution)/shard_map/reshape | solution.py:517
  1.4 0.0 copy-start
  1.4 0.9 %copy-done = f32[8,64,64]{2,1,0:T(8,128)S(1)} copy-done((f32[8,64,64]{2,1,0:T(8,128)S(1)}, f32[8,64,64]{2,1,0:T(8,128)}, u32[]{:S(2)}) %copy-start) | copy-done | bytes 131096
  2.3 0.0 copy-start.1
  2.3 0.7 %copy-done.1 = s32[256]{0:T(256)S(1)} copy-done((s32[256]{0:T(256)S(1)}, s32[256]{0:T(256)}, u32[]{:S(2)}) %copy-start.1) | copy-done | bytes 1048
  3.0 0.0 copy-start.2
  3.0 0.7 %copy-done.2 = s32[128]{0:T(128)S(1)} copy-done((s32[128]{0:T(128)S(1)}, s32[128]{0:T(128)}, u32[]{:S(2)}) %copy-start.2) | copy-done | bytes 536
  3.7 36.9 %shard_map.121 = (f32[32,16,512]{2,1,0:T(8,128)S(1)}, f32[32,16,512]{2,1,0:T(8,128)S(1)}, f32[8,128]{1,0:T(8,128)S(1)}) custom-call(s32[128]{0:T(128)S(1)} %copy-done.2, s32[256]{0:T(256)S(1)} %copy-done.1, s32[32,4]{1,0:T(8,128)S(1)} %copy.13.rows_s, f32[8,64,64]{2,1,0:T(8,128)S(1)} %copy-done, f32[32,16,512]{2,1,0:T(8,128)} %p_now_h.1, ...), custom_call_target="tpu_custom_call" | custom-call | tf_op jit(solution)/shard_map/pallas_call | solution.py:475
  40.6 1.0 %copy.17 = f32[32,16,512]{2,1,0:T(8,128)} copy(f32[32,16,512]{2,1,0:T(8,128)S(1)} %get-tuple-element.6) | data formatting | bytes 2097152
  41.5 1.0 %copy.18 = f32[32,16,512]{2,1,0:T(8,128)} copy(f32[32,16,512]{2,1,0:T(8,128)S(1)} %get-tuple-element.7) | data formatting | bytes 2097152
  42.5 0.6 %copy.19 = f32[8,128]{1,0:T(8,128)} copy(f32[8,128]{1,0:T(8,128)S(1)} %get-tuple-element.8) | data formatting | bytes 8192
Async XLA Ops:
  1.4 0.9 %copy-start = (f32[8,64,64]{2,1,0:T(8,128)S(1)}, f32[8,64,64]{2,1,0:T(8,128)}, u32[]{:S(2)}) copy-start(f32[8,64,64]{2,1,0:T(8,128)} %maps.1) | copy-start | bytes 393220
  2.3 0.7 %copy-start.1 = (s32[256]{0:T(256)S(1)}, s32[256]{0:T(256)}, u32[]{:S(2)}) copy-start(s32[256]{0:T(256)} %material_s.1) | copy-start | bytes 3076
  3.0 0.7 %copy-start.2 = (s32[128]{0:T(128)S(1)}, s32[128]{0:T(128)}, u32[]{:S(2)}) copy-start(s32[128]{0:T(128)} %patch_s.1) | copy-start | bytes 1540

commit v2 on v1

--- a/solution.py
+++ b/solution.py
@@ -36,9 +36,11 @@
     load_sem, chunk_sem, send_sem, recv_sem,
     info_ssem, info_rsem, relay_ssem, relay_rsem, grad_ssem, grad_rsem,
 ):
-    cz, blocks, cx, _ = speed2.shape
+    _, blocks, cx, _ = speed2.shape
+    cz = p_out.shape[0]
     devices, cap = rows_s.shape
     slots = devices * cap
+    plane = blocks * cx
     mats, depth, _ = maps.shape
     patches = material_s.shape[0]
     own = patches // devices
@@ -62,7 +64,7 @@
         loads[name] = [
             pltpu.make_async_copy(
                 src.at[:, :, pl.ds(rb * LANES, LANES)],
-                dst.at[:, rb] if name == "s" else dst.at[pl.ds(1, cz), rb],
+                dst.at[pl.ds(0 if name == "s" else 1, cz), rb],
                 load_sem.at[i, rb],
             )
             for rb in range(blocks)
@@ -203,7 +205,7 @@
             for step in range(STEPS):
                 for field in range(2):
                     if d < 2:
-                        x_recv[step, field, d] = jnp.zeros((cz, blocks, LANES), F32)
+                        x_recv[step, field, d] = jnp.zeros((cz * blocks, LANES), F32)
                     else:
                         z_recv[step, field, d - 2] = jnp.zeros((blocks, cx, LANES), F32)
 
@@ -211,32 +213,15 @@
         for copy in loads[name]:
             copy.wait()
 
-        @pl.loop(0, cz)
-        def _(z, name=name):
-            for rb in range(blocks):
-                x_send[0, which[name], 0, z, rb : rb + 1, :] = now[name][z + 1, rb, 0:1, :]
-                x_send[0, which[name], 1, z, rb : rb + 1, :] = now[name][z + 1, rb, cx - 1 : cx, :]
-
-    pl.semaphore_wait(barrier, devices - 1)
-    start_halo("a", 0, now["a"])
-    start_halo("p", 0, now["p"])
-
-    @pl.loop(1, devices)
-    def _(o):
-        k = lax.rem(me + o, devices)
-        pltpu.make_async_remote_copy(
-            src_ref=info_send.at[k], dst_ref=info_recv.at[me],
-            send_sem=info_ssem, recv_sem=info_rsem,
-            device_id=where_is(k), device_id_type=MESH,
-        ).start()
-
-    def relay_copy(k, part):
-        rows = pl.ds(0, 1) if part == 0 else pl.ds(1, TERMS - 1)
-        return pltpu.make_async_remote_copy(
-            src_ref=relay_send.at[k, rows], dst_ref=relay_recv.at[me, rows],
-            send_sem=relay_ssem.at[part], recv_sem=relay_rsem.at[part],
-            device_id=where_is(k), device_id_type=MESH,
-        )
+        flat = now[name].reshape((cz + 2) * plane, LANES)
+        for d, x in ((0, 0), (1, cx - 1)):
+            for b in range(cz * blocks // 8):
+                x_send[0, which[name], d, 8 * b : 8 * b + 8, :] = flat[
+                    pl.ds(plane + 8 * b * cx + x, 8, stride=cx), :
+                ]
+        for ref in buffers[name]:
+            ref[0] = jnp.zeros((blocks, cx, LANES), F32)
+            ref[cz + 1] = jnp.zeros((blocks, cx, LANES), F32)
 
     @pl.loop(0, chunks)
     def _(j):
@@ -259,12 +244,32 @@
                     relay_send[
                         chunk * peers + slot // cap, n, slot % cap : slot % cap + 1, :
                     ] = got[n : n + 1]
-        for q in range(peers):
-            k = chunk * peers + q
-            @pl.when(k != me)
-            def _(k=k):
-                relay_copy(k, 0).start()
-                relay_copy(k, 1).start()
+
+    pl.semaphore_wait(barrier, devices - 1)
+    start_halo("a", 0, now["a"])
+    start_halo("p", 0, now["p"])
+
+    @pl.loop(1, devices)
+    def _(o):
+        k = lax.rem(me + o, devices)
+        pltpu.make_async_remote_copy(
+            src_ref=info_send.at[k], dst_ref=info_recv.at[me],
+            send_sem=info_ssem, recv_sem=info_rsem,
+            device_id=where_is(k), device_id_type=MESH,
+        ).start()
+
+    def relay_copy(k, part):
+        rows = pl.ds(part, 1) if part < 2 else pl.ds(2, TERMS - 2)
+        return pltpu.make_async_remote_copy(
+            src_ref=relay_send.at[k, rows], dst_ref=relay_recv.at[me, rows],
+            send_sem=relay_ssem.at[part], recv_sem=relay_rsem.at[part],
+            device_id=where_is(k), device_id_type=MESH,
+        )
+
+    for part in range(3):
+        @pl.loop(1, devices)
+        def _(o, part=part):
+            relay_copy(lax.rem(me + o, devices), part).start()
 
     def gather(source, name, step):
         field = which[name]
@@ -291,13 +296,13 @@
             scale[n] = jnp.broadcast_to(info[:, n : n + 1], (slots, LANES))
 
     def wait_relay(part):
-        rows = pl.ds(0, 1) if part == 0 else pl.ds(1, TERMS - 1)
+        rows = pl.ds(part, 1) if part < 2 else pl.ds(2, TERMS - 2)
         side = relay_recv.at[pl.ds(0, devices - 1), rows]
         pltpu.make_async_remote_copy(
             src_ref=side, dst_ref=side, send_sem=relay_ssem.at[part], recv_sem=relay_rsem.at[part],
             device_id=where_is(lax.rem(me + 1, devices)), device_id_type=MESH,
         ).wait_recv()
-        for n in ([0] if part == 0 else range(1, TERMS)):
+        for n in ([part] if part < 2 else range(2, TERMS)):
             relay_recv[me, n] = relay_send[me, n]
             for k in range(devices):
                 surf[n, k * cap : (k + 1) * cap, :] = relay_recv[k, n]
@@ -356,52 +361,29 @@
     row_id = lax.broadcasted_iota(jnp.int32, (cx, LANES), 0)
     lane_id = lax.broadcasted_iota(jnp.int32, (cx, LANES), 1)
 
-    gather(now["a"], "a", 0)
-    wait_info()
-    gather(now["p"], "p", 0)
-    waited = {"ap": False, "s": False, "pp": False}
-    gathered = {("a", 0), ("p", 0)}
-    sent = False
-
-    for step, name in [(step, name) for step in range(STEPS) for name in ("a", "p")]:
-        field = which[name]
+    waited = set()
+
+    def need(*names):
+        for item in names:
+            if item not in waited:
+                waited.add(item)
+                for copy in loads[item]:
+                    copy.wait()
+
+    def fields(name, step):
+        ring = buffers[name]
+        return ring[step % 3], ring[(step + 1) % 3], ring[(step + 2) % 3]
+
+    def around(f, rb, right, left, lo, hi):
+        west = jnp.where(row_id == 0, lo, pltpu.roll(f[rb], 1, 0))
+        east = jnp.where(row_id == cx - 1, hi, pltpu.roll(f[rb], cx - 1, 0))
+        south = jnp.where(lane_id == 0, right[rb - 1] if rb else 0.0, right[rb])
+        north = jnp.where(lane_id == LANES - 1, left[rb + 1] if rb < blocks - 1 else 0.0, left[rb])
+        return (west + east) + (south + north)
+
+    def stencil(name, step):
+        earlier, current, result = fields(name, step)
         last = step == STEPS - 1
-        ring = buffers[name]
-        earlier, current = ring[step % 3], ring[(step + 1) % 3]
-        result = outs[name] if last else ring[(step + 2) % 3]
-
-        if name == "p" and step < 2:
-            wait_relay(step)
-        if last and name == "a":
-            correlate()
-        if last and name == "p":
-            back = backs[step]
-        else:
-            back = back_rows(name, step)
-        if name == "p":
-            backs[step] = back
-        delta = BETA * (back - hist[field, step])
-        both = jnp.concatenate(split(delta), axis=0)
-
-        @pl.loop(0, 4, unroll=True)
-        def _(part):
-            span = pl.ds(pl.multiple_of(part * (cz // 4), cz // 4), cz // 4)
-            couple[span] = jnp.dot(
-                spread[span].reshape(cz // 4 * blocks * cx, 2 * slots), both,
-                preferred_element_type=F32,
-            ).reshape(cz // 4, blocks, cx, LANES)
-
-        for need in ((name + "p",) if step == 0 else ()) + ("s",):
-            if not waited[need]:
-                waited[need] = True
-                for copy in loads[need]:
-                    copy.wait()
-        wait_recv(name, step)
-        if step > 0:
-            wait_send(name, step - 1, earlier)
-
-        current[0] = z_recv[step, field, 0]
-        current[cz + 1] = z_recv[step, field, 1]
 
         @pl.loop(0, cz, unroll=UNROLL)
         def _(z):
@@ -409,30 +391,87 @@
             right = [pltpu.roll(part, 1, 1) for part in f]
             left = [pltpu.roll(part, LANES - 1, 1) for part in f]
             for rb in range(blocks):
-                lo = x_recv[step, field, 0, z, rb : rb + 1, :]
-                hi = x_recv[step, field, 1, z, rb : rb + 1, :]
-                west = jnp.where(row_id == 0, lo, pltpu.roll(f[rb], 1, 0))
-                east = jnp.where(row_id == cx - 1, hi, pltpu.roll(f[rb], cx - 1, 0))
-                south = jnp.where(lane_id == 0, right[rb - 1] if rb else 0.0, right[rb])
-                north = jnp.where(
-                    lane_id == LANES - 1, left[rb + 1] if rb < blocks - 1 else 0.0, left[rb]
-                )
-                beside = (current[z, rb] + current[z + 2, rb]) + (west + east) + (south + north)
-                new = (2.0 * f[rb] - earlier[z + 1, rb] + couple[z, rb]) + speed2[z, rb] * (
-                    beside - 6.0 * f[rb]
-                )
+                lo, hi = 0.0, 0.0
                 if last:
-                    result[z, :, rb * LANES : (rb + 1) * LANES] = new
+                    lo = x_recv[step, which[name], 0, pl.ds(z * blocks + rb, 1), :]
+                    hi = x_recv[step, which[name], 1, pl.ds(z * blocks + rb, 1), :]
+                beside = (current[z, rb] + current[z + 2, rb]) + around(f, rb, right, left, lo, hi)
+                new = (2.0 * f[rb] - earlier[z + 1, rb]) + speed2[z, rb] * (beside - 6.0 * f[rb])
+                if last:
+                    outs[name][z, :, rb * LANES : (rb + 1) * LANES] = new + couple[z, rb]
                 else:
                     result[z + 1, rb] = new
-                    x_send[step + 1, field, 0, z, rb : rb + 1, :] = new[0:1]
-                    x_send[step + 1, field, 1, z, rb : rb + 1, :] = new[cx - 1 : cx]
-
-        if last:
-            wait_send(name, step, current)
+
+    def couplings(name, step):
+        if step == STEPS - 1 and name == "p":
+            back = backs[step]
         else:
-            start_halo(name, step + 1, result)
-            gather(result, name, step + 1)
+            back = back_rows(name, step)
+        if name == "p":
+            backs[step] = back
+        delta = BETA * (back - hist[which[name], step])
+        both = jnp.concatenate(split(delta), axis=0)
+        result = fields(name, step)[2]
+        size = cz // 4
+        for part in range(4):
+            at = part * size
+            extra = jnp.dot(
+                spread[at : at + size].reshape(size * plane, 2 * slots), both,
+                preferred_element_type=F32,
+            ).reshape(size, blocks, cx, LANES)
+            if step == STEPS - 1:
+                couple[at : at + size] = extra
+            else:
+                result[at + 1 : at + 1 + size] = result[at + 1 : at + 1 + size] + extra
+
+    def finish(name, step):
+        field = which[name]
+        earlier, current, result = fields(name, step)
+        wait_recv(name, step)
+        if step > 0:
+            wait_send(name, step - 1, earlier)
+        result[1] = result[1] + speed2[0] * z_recv[step, field, 0]
+        result[cz] = result[cz] + speed2[cz - 1] * z_recv[step, field, 1]
+        flat = result.reshape((cz + 2) * plane, LANES)
+        gain = speed2.reshape((cz + 1) * plane, LANES)
+        for d, x in ((0, 0), (1, cx - 1)):
+            for b in range(cz * blocks // 8):
+                at = 8 * b * cx + x
+                new = flat[pl.ds(plane + at, 8, stride=cx), :] + (
+                    gain[pl.ds(at, 8, stride=cx), :]
+                    * x_recv[step, field, d, 8 * b : 8 * b + 8, :]
+                )
+                flat[pl.ds(plane + at, 8, stride=cx), :] = new
+                x_send[step + 1, field, d, 8 * b : 8 * b + 8, :] = new
+        start_halo(name, step + 1, result)
+        gather(result, name, step + 1)
+
+    gather(now["a"], "a", 0)
+    gather(now["p"], "p", 0)
+    for step in range(STEPS - 1):
+        need("ap", "s")
+        stencil("a", step)
+        need("pp")
+        stencil("p", step)
+        if step == 0:
+            wait_info()
+        couplings("a", step)
+        finish("a", step)
+        wait_relay(step)
+        couplings("p", step)
+        finish("p", step)
+    correlate()
+    step = STEPS - 1
+    for name in ("a", "p"):
+        couplings(name, step)
+        earlier, current, result = fields(name, step)
+        wait_recv(name, step)
+        wait_send(name, step - 1, earlier)
+        current[0] = z_recv[step, which[name], 0]
+        current[cz + 1] = z_recv[step, which[name], 1]
+        stencil(name, step)
+    for name in ("a", "p"):
+        wait_send(name, step, fields(name, step)[1])
 
     side = grad_recv.at[pl.ds(0, devices - 1)]
     pltpu.make_async_remote_copy(
@@ -445,7 +484,8 @@
         (0, grad_ssem, grad_send.at[pl.ds(0, devices - 1)]),
         (0, info_ssem, info_send.at[pl.ds(0, devices - 1)]),
         (0, relay_ssem.at[0], relay_send.at[pl.ds(0, devices - 1), pl.ds(0, 1)]),
-        (1, relay_ssem.at[1], relay_send.at[pl.ds(0, devices - 1), pl.ds(1, TERMS - 1)]),
+        (1, relay_ssem.at[1], relay_send.at[pl.ds(0, devices - 1), pl.ds(1, 1)]),
+        (2, relay_ssem.at[2], relay_send.at[pl.ds(0, devices - 1), pl.ds(2, TERMS - 2)]),
     ):
         pltpu.make_async_remote_copy(
             src_ref=buf, dst_ref=buf, send_sem=sem, recv_sem=grad_rsem,
@@ -470,6 +510,7 @@
     dma = pltpu.SemaphoreType.DMA
     blocks = ny // LANES
     tile = pltpu.VMEM((cz, blocks, cx, LANES), F32)
+    gain = pltpu.VMEM((cz + 1, blocks, cx, LANES), F32)
     halo = pltpu.VMEM((cz + 2, blocks, cx, LANES), F32)
     rows = pltpu.VMEM((devices, cap, width), F32)
     return pl.pallas_call(
@@ -482,7 +523,7 @@
         in_specs=[smem] * 3 + [vmem] + [hbm] * 6,
         out_specs=(vmem, vmem, vmem),
         scratch_shapes=[
-            halo, halo, halo, halo, halo, halo, tile,
+            halo, halo, halo, halo, halo, halo, gain,
             pltpu.VMEM((slots, depth, width), F32),
             pltpu.VMEM((cz, blocks, cx, 2 * slots), BF16),
             tile,
@@ -503,12 +544,12 @@
             pltpu.VMEM((TERMS, slots, width), F32),
             pltpu.VMEM((devices, own, width), F32),
             pltpu.VMEM((devices, own, width), F32),
-            pltpu.VMEM((STEPS, 2, 2, cz, blocks, LANES), F32),
-            pltpu.VMEM((STEPS, 2, 2, cz, blocks, LANES), F32),
+            pltpu.VMEM((STEPS, 2, 2, cz * blocks, LANES), F32),
+            pltpu.VMEM((STEPS, 2, 2, cz * blocks, LANES), F32),
             pltpu.VMEM((STEPS, 2, 2, blocks, cx, LANES), F32),
             dma((5, blocks)), dma((slots // CHUNK,)),
             dma((STEPS, 2, 4)), dma((STEPS, 2, 4)),
-            dma, dma, dma((2,)), dma((2,)), dma, dma,
+            dma, dma, dma((3,)), dma((3,)), dma, dma,
         ],
         compiler_params=pltpu.CompilerParams(
             collective_id=0, has_side_effects=True, vmem_limit_bytes=51 * 1024 * 1024

time: 43.3 us -> 39.1 us (0.903)
  Pallas kernels: 36.9 us -> 32.7 us
    pallas_call x1, Pallas kernels: 36.9 us -> 32.7 us  [body(): pl.pallas_call(functools.partial(kernel_body, nx, nz), out_shape=(jax.Sha...]
where the time goes in v2:
time: 39.1 us; the launch traced here: 38.9 us
  Pallas kernels  32.7 us (84%)
  local copies, waits for them, and re-layouts  5.58 us (14%)
  between operations  0.64 us (2%)
    pallas_call x1, Pallas kernels, body(): pl.pallas_call(functools.partial(kernel_body, nx, nz), out_shape=(jax.Sha...  32.7 us
    unnamed x9, local copies, waits for them, and re-layouts  4.82 us

profile of v2, /device:TPU:0, one launch (start us, length us, event | category | flops | bytes accessed | tf_op | source)
XLA Modules:
  0.0 38.9 jit_solution(5153751766268323579)
XLA Ops:
  0.6 0.8 %copy.13.rows_s = s32[32,4]{1,0:T(8,128)S(1)} copy(s32[32,4]{0,1:T(4,128)} %bitcast.1) | data formatting | bytes 1024 | tf_op jit(solution)/shard_map/reshape | solution.py:558
  1.4 0.0 copy-start
  1.4 0.9 %copy-done = f32[8,64,64]{2,1,0:T(8,128)S(1)} copy-done((f32[8,64,64]{2,1,0:T(8,128)S(1)}, f32[8,64,64]{2,1,0:T(8,128)}, u32[]{:S(2)}) %copy-start) | copy-done | bytes 131096
  2.3 0.0 copy-start.1
  2.3 0.7 %copy-done.1 = s32[256]{0:T(256)S(1)} copy-done((s32[256]{0:T(256)S(1)}, s32[256]{0:T(256)}, u32[]{:S(2)}) %copy-start.1) | copy-done | bytes 1048
  3.0 0.0 copy-start.2
  3.0 0.7 %copy-done.2 = s32[128]{0:T(128)S(1)} copy-done((s32[128]{0:T(128)S(1)}, s32[128]{0:T(128)}, u32[]{:S(2)}) %copy-start.2) | copy-done | bytes 536
  3.7 32.7 %shard_map.121 = (f32[32,16,512]{2,1,0:T(8,128)S(1)}, f32[32,16,512]{2,1,0:T(8,128)S(1)}, f32[8,128]{1,0:T(8,128)S(1)}) custom-call(s32[128]{0:T(128)S(1)} %copy-done.2, s32[256]{0:T(256)S(1)} %copy-done.1, s32[32,4]{1,0:T(8,128)S(1)} %copy.13.rows_s, f32[8,64,64]{2,1,0:T(8,128)S(1)} %copy-done, f32[32,16,512]{2,1,0:T(8,128)} %p_now_h.1, ...), custom_call_target="tpu_custom_call" | custom-call | tf_op jit(solution)/shard_map/pallas_call | solution.py:516
  36.4 1.0 %copy.17 = f32[32,16,512]{2,1,0:T(8,128)} copy(f32[32,16,512]{2,1,0:T(8,128)S(1)} %get-tuple-element.6) | data formatting | bytes 2097152
  37.3 1.0 %copy.18 = f32[32,16,512]{2,1,0:T(8,128)} copy(f32[32,16,512]{2,1,0:T(8,128)S(1)} %get-tuple-element.7) | data formatting | bytes 2097152
  38.3 0.6 %copy.19 = f32[8,128]{1,0:T(8,128)} copy(f32[8,128]{1,0:T(8,128)S(1)} %get-tuple-element.8) | data formatting | bytes 8192
Async XLA Ops:
  1.4 0.9 %copy-start = (f32[8,64,64]{2,1,0:T(8,128)S(1)}, f32[8,64,64]{2,1,0:T(8,128)}, u32[]{:S(2)}) copy-start(f32[8,64,64]{2,1,0:T(8,128)} %maps.1) | copy-start | bytes 393220
  2.3 0.7 %copy-start.1 = (s32[256]{0:T(256)S(1)}, s32[256]{0:T(256)}, u32[]{:S(2)}) copy-start(s32[256]{0:T(256)} %material_s.1) | copy-start | bytes 3076
  3.0 0.7 %copy-start.2 = (s32[128]{0:T(128)S(1)}, s32[128]{0:T(128)}, u32[]{:S(2)}) copy-start(s32[128]{0:T(128)} %patch_s.1) | copy-start | bytes 1540
